TPU v7x, 1024 devices: a whole 8x8x8 slice. The times are simulated.
1024 devices in a mesh: row: 64 (over y, x_lo, core), col: 16 (over z, x_hi).
Axes of the slice: x: 8 (x_hi: 2, x_lo: 4; x = x_hi * 4 + x_lo), y: 8, z: 8, core: 2. Of those that a mesh axis runs over, the one named last changes fastest.
Arguments:
- field: bfloat16 [64, 1536, 2, 2, 512], P(None, 'row', None, None, 'col'), may hold values from -6 to 6
- coef: float32 [1536, 512], P('row', 'col'), may hold values from 0.3 to 3
- table: bfloat16 [64, 1024, 1536], P('row'), may hold values from -0.15625 to 0.15625
- order_ids: int32 [64], P('row'), may hold values from 0 to 1023, as said below
- inverses: bfloat16 [1024, 512, 512], P(('row', 'col')), may hold values from -0.25 to 0.25
- degree_owner: int32 [1024], replicated, may hold values from 0 to 1023, each once
Outputs:
- synthesized: bfloat16 [64, 1536, 2, 2, 512], P(None, 'row', None, None, 'col')
Inputs may be any that keep to these rules, and one draw needn't show every extreme that they name: `order_ids`: distinct orders; 0 and 1023 are always among them. `degree_owner`: every degree appears exactly once.
All inputs are finite; a program needn't handle non-finite values.
Results may differ from a plain program's by a relative error of at most 0.0064.
Values may be sent and summed in bfloat16 or wider, within the bound.
A program may use at most 32 MiB of HBM per device.

v0:
```python
import jax
import jax.numpy as jnp
from jax import lax
from jax.sharding import PartitionSpec as P


def analyze(degree_table, order_id, columns, block_rows):
    degrees_all = degree_table.shape[0]

    def analyze_add_block(block_no, spectra):
        first_row = block_no * block_rows
        table_part = lax.dynamic_slice_in_dim(degree_table, first_row, block_rows, 0)
        product = jnp.dot(table_part, columns, preferred_element_type=jnp.float32)
        degree = first_row + lax.iota(jnp.int32, block_rows)
        product = jnp.where((degree >= order_id)[:, None], product, 0.0)
        return lax.dynamic_update_slice_in_dim(spectra, product.astype(jnp.bfloat16), first_row, 0)

    blank_rows = jnp.zeros((degrees_all, columns.shape[1]), jnp.bfloat16)
    return lax.fori_loop(
        order_id // block_rows, degrees_all // block_rows, analyze_add_block, blank_rows
    )


def synthesize(degree_table, order_id, coeffs, block_rows):
    degrees_all = degree_table.shape[0]

    def synthesize_add_block(block_no, running):
        first_row = block_no * block_rows
        table_part = lax.dynamic_slice_in_dim(degree_table, first_row, block_rows, 0)
        coeff_part = lax.dynamic_slice_in_dim(coeffs, first_row, block_rows, 0)
        return running + lax.dot_general(
            table_part, coeff_part, (((0,), (0,)), ((), ())), preferred_element_type=jnp.float32
        )

    zero_sum = jnp.zeros((degree_table.shape[1], coeffs.shape[1]), jnp.float32)
    return lax.fori_loop(
        order_id // block_rows, degrees_all // block_rows, synthesize_add_block, zero_sum
    ).astype(jnp.bfloat16)


def per_device(field, coef, table, order_ids, inverses, degree_owner):
    ord_dev = table.shape[0]
    degrees_all = table.shape[1]
    latitudes = table.shape[2]
    members = field.shape[2]
    radii_dev = field.shape[4]
    block_rows = 128
    weighted = (field.astype(jnp.float32) * coef[None, :, None, None, :]).astype(jnp.bfloat16)
    arrived_all = lax.all_to_all(weighted, "row", split_axis=0, concat_axis=1, tiled=True)
    spectral = jnp.stack(
        [analyze(table[0], order_ids[0], arrived_all[0].reshape(latitudes, -1), block_rows)]
    )
    spectral = spectral.reshape(ord_dev, degrees_all, members, 2, radii_dev)
    positions = lax.iota(jnp.int32, degrees_all)
    placed = jnp.take(spectral, degree_owner, axis=1)
    owned_rows = lax.all_to_all(
        lax.all_to_all(placed, "row", split_axis=1, concat_axis=0, tiled=True),
        "col",
        split_axis=1,
        concat_axis=4,
        tiled=True,
    )
    solved = jnp.einsum(
        "kdfcs,drs->kdfcr", owned_rows, inverses, preferred_element_type=jnp.float32
    ).astype(jnp.bfloat16)
    returned = lax.all_to_all(
        lax.all_to_all(solved, "col", split_axis=4, concat_axis=1, tiled=True),
        "row",
        split_axis=0,
        concat_axis=1,
        tiled=True,
    )
    inverse_order = jnp.zeros((degrees_all,), jnp.int32).at[degree_owner].set(positions)
    coeffs = jnp.take(returned, inverse_order, axis=1)
    outputs = jnp.stack(
        [synthesize(table[0], order_ids[0], coeffs[0].reshape(degrees_all, -1), block_rows)]
    )
    outputs = outputs.reshape(ord_dev, latitudes, members, 2, radii_dev)
    return lax.all_to_all(outputs, "row", split_axis=1, concat_axis=0, tiled=True)


def solution(mesh):
    in_specs = (
        P(None, "row", None, None, "col"),
        P("row", "col"),
        P("row", None, None),
        P("row"),
        P(("row", "col"), None, None),
        P(),
    )
    out_specs = P(None, "row", None, None, "col")
    return jax.shard_map(
        per_device, mesh=mesh, in_specs=in_specs, out_specs=out_specs, check_vma=False
    )
```

profile of v0, /device:TPU:1, one launch (start us, length us, event | category | flops | bytes accessed | tf_op | source)
XLA Modules:
  0.0 219.9 jit_solution(3909988211275341401)
XLA Ops:
  0.0 0.0 copy-start
  0.0 2.3 %copy.49 = bf16[64,24,2,2,32]{4,1,3,2,0:T(8,128)(2,1)S(1)} copy(bf16[64,24,2,2,32]{0,4,3,2,1:T(8,128)(2,1)} %param.12) | data formatting | bytes 786432 | tf_op args[0]
  2.3 0.0 copy-start.1
  2.3 2.2 fusion.12
  4.5 3.5 %reshape.85 = bf16[64,2,1536]{2,1,0:T(2,128)(2,1)} reshape(bf16[64,2,2,24,32]{4,3,2,1,0:T(8,128)(2,1)} %fusion.12) | data formatting | bytes 786432
  8.1 18.2 %all-to-all-start = ((bf16[64,2,1536]{2,1,0:T(2,128)(2,1)}), bf16[64,2,1536]{2,1,0:T(2,128)(2,1)S(1)}, u32[]{:S(2)}, u32[]{:S(2)}) async-start(bf16[64,2,1536]{2,1,0:T(2,128)(2,1)} %reshape.85), calls=%async_computation | async-start | bytes 786432 | tf_op jit(solution)/shard_map/all_to_all | solution.py:49
  26.9 0.0 copy-done.1
  27.0 15.5 %all-to-all-done = bf16[64,2,1536]{2,1,0:T(2,128)(2,1)S(1)} async-done(((bf16[64,2,1536]{2,1,0:T(2,128)(2,1)}), bf16[64,2,1536]{2,1,0:T(2,128)(2,1)S(1)}, u32[]{:S(2)}, u32[]{:S(2)}) %all-to-all-start) | async-done | bytes 393248 | tf_op jit(solution)/shard_map/all_to_all | solution.py:49
  42.4 0.8 reshape.86
  43.3 2.4 %copy.50 = bf16[64,24,2,2,32]{4,3,2,1,0:T(2,128)(2,1)} copy(bf16[64,24,2,2,32]{4,1,3,2,0:T(8,128)(2,1)S(1)} %bitcast.69) | data formatting | bytes 786432 | tf_op jit(solution)/shard_map/all_to_all | solution.py:49
  45.7 3.7 %reshape_squeeze.6 = bf16[1536,128]{1,0:T(8,128)(2,1)S(1)} reshape(bf16[64,24,2,2,32]{4,3,2,1,0:T(2,128)(2,1)} %copy.50) | data formatting | bytes 786432 | tf_op jit(solution)/shard_map/reshape;squeeze | solution.py:51
  49.4 8.3 %while.20 = (s32[]{:T(128)}, bf16[1024,128]{0,1:T(8,128)(2,1)S(1)}, s32[]{:T(128)}, bf16[1024,1536]{1,0:T(8,128)(2,1)}, bf16[1536,128]{1,0:T(8,128)(2,1)S(1)}, /*index=5*/s32[]{:T(128)}, s32[]{:T(128)}, s32[]{:T(128)}, s32[]{:T(128)}) while((s32[]{:T(128)}, bf16[1024,128]{0,1:T(8,128)(2,1)S(1)}, s32[]{:T(128)}, bf16[1024,1536]{1,0:T(8,128)(2,1)}, ...), condition=%wide.region_1.2_spmd, body=%wide.region_0.1_spmd.sunk | while | flops 50364676 | bytes 950683 | solution.py:19
  49.4 0.7 add_compare_fusion.2
  50.1 1.3 fusion.23
  51.4 0.1 copy.78
  51.5 0.7 add_compare_fusion.2
  52.2 1.3 fusion.23
  53.4 0.1 copy.78
  53.6 0.7 add_compare_fusion.2
  54.3 1.3 fusion.23
  55.5 0.1 copy.78
  55.7 0.7 add_compare_fusion.2
  56.3 1.3 fusion.23
  57.6 0.1 copy.78
  57.8 0.8 copy.52
  58.5 4.8 %gather_fusion = bf16[1024,2,2,32]{3,2,1,0:T(2,128)(2,1)S(1)} fusion(bf16[1024,2,2,32]{3,2,1,0:T(2,128)(2,1)S(1)} %bitcast.75, s32[1024]{0:T(1024)S(1)} %get-tuple-element.91), kind=kCustom, calls=%fused_computation.clone | custom fusion | bytes 528384 | tf_op jit(solution)/shard_map/jit(_take)/gather | solution.py:55
  63.4 3.8 %fusion.13 = bf16[1024,1,2,2,32]{4,3,2,1,0:T(2,128)(2,1)S(1)} fusion(bf16[1024,2,2,32]{3,2,1,0:T(2,128)(2,1)S(1)} %gather_fusion, pred[1024]{0:T(1024)(128)(4,1)S(1)} %compare_and_fusion.1), kind=kLoop, calls=%fused_computation.29 | loop fusion | flops 131072 | bytes 525312
  67.2 1.0 reshape.87
  68.2 25.9 %all_to_all.78 = bf16[64,2,1024]{2,1,0:T(2,128)(2,1)S(1)} all-to-all(bf16[64,2,1024]{2,1,0:T(2,128)(2,1)S(1)} %reshape.87), channel_id=1, replica_groups=mesh['row'=64,'col'=16] {'row'}, dimensions={0} | all-to-all | bytes 524288 | tf_op jit(solution)/shard_map/all_to_all | solution.py:57
  94.1 0.5 reshape.88
  94.6 1.2 copy.55
  95.8 0.4 reshape.89
  96.2 25.4 %all_to_all.79 = bf16[16,2,4096]{2,1,0:T(2,128)(2,1)S(1)} all-to-all(bf16[16,2,4096]{2,1,0:T(2,128)(2,1)S(1)} %reshape.89), channel_id=1, replica_groups=mesh['row'=64,'col'=16] {'col'}, dimensions={0} | all-to-all | bytes 524288 | tf_op jit(solution)/shard_map/all_to_all | solution.py:56
  121.6 0.3 reshape.90
  122.1 0.0 copy-done
  122.1 0.5 fusion.6
  122.6 0.4 copy.58
  123.0 0.4 reshape.91
  123.4 18.4 %all_to_all.80 = bf16[16,2,4096]{2,1,0:T(2,128)(2,1)S(1)} all-to-all(bf16[16,2,4096]{2,1,0:T(2,128)(2,1)S(1)} %reshape.91), channel_id=1, replica_groups=mesh['row'=64,'col'=16] {'col'}, dimensions={0} | all-to-all | bytes 524288 | tf_op jit(solution)/shard_map/all_to_all | solution.py:67
  141.8 0.3 reshape.92
  142.2 0.1 copy.59
  142.2 1.6 copy.60
  143.8 1.7 reshape.93
  145.5 7.2 %all-to-all-start.4 = ((bf16[64,2,1024]{2,1,0:T(2,128)(2,1)}), bf16[64,2,1024]{2,1,0:T(2,128)(2,1)S(1)}, u32[]{:S(2)}, u32[]{:S(2)}) async-start(bf16[64,2,1024]{2,1,0:T(2,128)(2,1)} %reshape.93), calls=%async_computation.4 | async-start | bytes 524288 | tf_op jit(solution)/shard_map/all_to_all | solution.py:66
  152.7 4.3 %scatter_custom_fusion = s32[1024]{0:T(1024)S(1)} fusion(s32[1024]{0:T(1024)S(1)} %get-tuple-element.92, s32[1024]{0:T(1024)S(1)} %iota.8, s32[]{:T(128)} %constant.50.clone.1), kind=kCustom, calls=%fused_computation.26 | custom fusion | bytes 4100 | tf_op jit(solution)/shard_map/scatter | solution.py:73
  157.1 9.1 %all-to-all-done.4 = bf16[64,2,1024]{2,1,0:T(2,128)(2,1)S(1)} async-done(((bf16[64,2,1024]{2,1,0:T(2,128)(2,1)}), bf16[64,2,1024]{2,1,0:T(2,128)(2,1)S(1)}, u32[]{:S(2)}, u32[]{:S(2)}) %all-to-all-start.4) | async-done | bytes 262176 | tf_op jit(solution)/shard_map/all_to_all | solution.py:66
  166.2 0.5 reshape.94
  166.7 1.1 copy.61
  167.8 8.5 %gather_fusion.1 = bf16[1024,2,2,32]{3,2,1,0:T(2,128)(2,1)} fusion(bf16[1024,2,2,32]{3,2,1,0:T(2,128)(2,1)S(1)} %bitcast.77, s32[1024]{0:T(1024)S(1)} %fusion.9), kind=kCustom, calls=%fused_computation.1.clone | custom fusion | bytes 528384 | tf_op jit(solution)/shard_map/jit(_take)/gather | solution.py:74
  176.3 5.3 %broadcast_select_fusion = bf16[1,1024,2,2,32]{4,3,2,1,0:T(2,128)(2,1)S(1)} fusion(pred[1024]{0:T(1024)(128)(4,1)S(1)} %compare_and_fusion, bf16[1024,2,2,32]{3,2,1,0:T(2,128)(2,1)} %gather_fusion.1), kind=kLoop, calls=%fused_computation.14 | loop fusion | flops 131072 | bytes 525312 | tf_op jit(solution)/shard_map/jit(_take)/select_n | solution.py:74
  181.6 1.3 copy.62
  183.0 0.1 broadcast_in_dim.32
  183.1 5.6 %while.21 = (s32[]{:T(128)}, f32[1536,128]{1,0:T(8,128)S(1)}, bf16[1024,1536]{1,0:T(8,128)(2,1)}, bf16[1024,128]{0,1:T(8,128)(2,1)S(1)}, s32[]{:T(128)}, /*index=5*/s32[]{:T(128)}, s32[]{:T(128)}, s32[]{:T(128)}) while((s32[]{:T(128)}, f32[1536,128]{1,0:T(8,128)S(1)}, bf16[1024,1536]{1,0:T(8,128)(2,1)}, bf16[1024,128]{0,1:T(8,128)(2,1)S(1)}, ...), condition=%wide.region_4.6_spmd, body=%wide.region_3.5_spmd.sunk | while | flops 50528260 | bytes 2000003 | solution.py:36
  183.1 1.3 convolution_add_fusion.2
  184.4 1.3 convolution_add_fusion.2
  185.8 1.3 convolution_add_fusion.2
  187.1 1.3 convolution_add_fusion.2
  188.6 0.2 copy.64
  188.8 1.1 copy.65
  189.9 1.1 reshape.95
  191.0 25.3 %all_to_all.81 = bf16[64,2,1536]{2,1,0:T(2,128)(2,1)S(1)} all-to-all(bf16[64,2,1536]{2,1,0:T(2,128)(2,1)S(1)} %reshape.95), channel_id=1, replica_groups=mesh['row'=64,'col'=16] {'row'}, dimensions={0} | all-to-all | bytes 786432 | tf_op jit(solution)/shard_map/all_to_all | solution.py:79
  216.4 0.8 reshape.96
  217.2 2.7 %copy.67 = bf16[64,24,2,2,32]{0,4,3,2,1:T(8,128)(2,1)} copy(bf16[64,24,2,2,32]{4,3,2,1,0:T(2,128)(2,1)S(1)} %bitcast.70) | data formatting | bytes 786432 | tf_op jit(solution)/shard_map/all_to_all | solution.py:79
  (12 shorter events, 0.2 us)
Async XLA Ops:
  0.0 122.1 %copy-start = (bf16[1,512,512]{2,1,0:T(8,128)(2,1)S(1)}, bf16[1,512,512]{2,1,0:T(8,128)(2,1)}, u32[]{:S(2)}) copy-start(bf16[1,512,512]{2,1,0:T(8,128)(2,1)} %param.16) | copy-start | bytes 1572868
  2.3 24.6 %copy-start.1 = (s32[1024]{0:T(1024)S(1)}, s32[1024]{0:T(1024)}, u32[]{:S(2)}) copy-start(s32[1024]{0:T(1024)} %param.17) | copy-start | bytes 12292
  8.1 34.4 %all-to-all-start = ((bf16[64,2,1536]{2,1,0:T(2,128)(2,1)}), bf16[64,2,1536]{2,1,0:T(2,128)(2,1)S(1)}, u32[]{:S(2)}, u32[]{:S(2)}) async-start(bf16[64,2,1536]{2,1,0:T(2,128)(2,1)} %reshape.85), calls=%async_computation | async-start | bytes 786432 | tf_op jit(solution)/shard_map/all_to_all | solution.py:49
  145.5 20.7 %all-to-all-start.4 = ((bf16[64,2,1024]{2,1,0:T(2,128)(2,1)}), bf16[64,2,1024]{2,1,0:T(2,128)(2,1)S(1)}, u32[]{:S(2)}, u32[]{:S(2)}) async-start(bf16[64,2,1024]{2,1,0:T(2,128)(2,1)} %reshape.93), calls=%async_computation.4 | async-start | bytes 524288 | tf_op jit(solution)/shard_map/all_to_all | solution.py:66
where the time goes:
time: 221 us; the launch traced here: 220 us
  blocking collectives  95.1 us (43%)
  local copies, waits for them, and re-layouts  48.6 us (22%)
  starting transfers between devices  25.4 us (11%)
  waiting for transfers between devices  24.6 us (11%)
  other arithmetic  14 us (6%)
  matrix products  10.8 us (5%)
    all_to_all x1, blocking collectives, per_device(): lax.all_to_all(placed, 'row', split_axis=1, concat_axis=0, tiled=True)  25.9 us
    all_to_all x1, blocking collectives, per_device(): lax.all_to_all(lax.all_to_all(placed, 'row', split_axis=1, concat_axis=0,...  25.4 us
    all_to_all x1, blocking collectives, per_device(): lax.all_to_all(outputs, 'row', split_axis=1, concat_axis=0, tiled=True)  25.3 us
    all_to_all x1, blocking collectives, per_device(): lax.all_to_all(solved, 'col', split_axis=4, concat_axis=1, tiled=True)  18.4 us
    all_to_all x1, starting transfers between devices, per_device(): lax.all_to_all(weighted, 'row', split_axis=0, concat_axis=1, tiled=True)  18.2 us
    all_to_all x1, waiting for transfers between devices, per_device(): lax.all_to_all(weighted, 'row', split_axis=0, concat_axis=1, tiled=True)  15.5 us
    unnamed x17, local copies, waits for them, and re-layouts  13.8 us
    all_to_all x1, waiting for transfers between devices, per_device(): lax.all_to_all(lax.all_to_all(solved, 'col', split_axis=4, concat_axis=1,...  9.14 us
  transfers between devices with their start and end apart: 2, of which 2 were waited for; matrix products, arithmetic and copies ran while one was open for 2% of the time, Pallas kernels for 0%

commit v1 on v0

v1 whole, which is shorter than its diff:
```python
import functools

import jax
import jax.numpy as jnp
from jax import lax
from jax.experimental import pallas as pl
from jax.experimental.pallas import tpu as pltpu
from jax.sharding import PartitionSpec as P

MESH = pl.DeviceIdType.MESH
BF = jnp.bfloat16
F32 = jnp.float32


class Plan:
    def __init__(self, rows, cols, lat, radii, members):
        self.rows, self.cols = rows, cols
        self.co = 2
        self.xl = 4 if rows % 32 == 0 else 2
        self.y = rows // (self.xl * self.co)
        self.na = self.y * self.co
        self.nb = cols * self.xl
        self.deg = rows * cols
        self.t = lat // rows
        self.rd = radii // cols
        self.fc = members
        self.j = members * self.rd


def kernel(pn, field, coef, table, inv, deg, order, out,
           fv, cv, tv, iv, dv, s1, r1, sf, perm, tp, tt, w, sp, e1, e2, d2, o2,
           g1, g2, h1, ob, vb, zv, insem, ssem, rsem):
    rows, cols, na, nb, nt, nj = pn.rows, pn.cols, pn.na, pn.nb, pn.t, pn.j
    me_row, me_col = lax.axis_index("row"), lax.axis_index("col")
    co = me_row % pn.co
    xl = (me_row // pn.co) % pn.xl
    y = me_row // (pn.co * pn.xl)
    me_a = y * pn.co + co
    me_b = me_col * pn.xl + xl

    def row_peer(s):
        j = (me_row + s) % rows
        return j, (j, me_col)

    def a_peer(s):
        a = (me_a + s) % na
        return a, (((a // pn.co) * pn.xl + xl) * pn.co + a % pn.co, me_col)

    def b_peer(s):
        b = (me_b + s) % nb
        return b, ((y * pn.xl + b % pn.xl) * pn.co + co, b // pn.xl)

    loads = [(field, fv), (coef, cv), (deg, dv), (table, tv), (inv, iv)]
    loads = [pltpu.make_async_copy(src, dst, insem.at[i]) for i, (src, dst) in enumerate(loads)]
    for c in loads:
        c.start()

    barrier = pltpu.get_barrier_semaphore()

    def greet(peer, s, _):
        pl.semaphore_signal(barrier, inc=1, device_id=peer(s)[1], device_id_type=MESH)
        return 0

    lax.fori_loop(1, rows, functools.partial(greet, row_peer), 0)
    lax.fori_loop(1, nb, functools.partial(greet, b_peer), 0)

    loads[0].wait()
    loads[1].wait()
    eye = (lax.broadcasted_iota(jnp.int32, (rows, rows), 0)
           == lax.broadcasted_iota(jnp.int32, (rows, rows), 1)).astype(F32).astype(BF)
    tc = 4
    for i in range(nt // tc):
        x = fv[pl.ds(i * tc, tc)].reshape(tc * nj, rows)
        yv = lax.dot_general(eye, x, (((1,), (1,)), ((), ())), preferred_element_type=F32)
        for t in range(tc):
            sf[pl.ds((i * tc + t) * rows, rows), :] = yv[:, t * nj:(t + 1) * nj]
    c4 = jnp.concatenate([cv[...]] * pn.fc, axis=1)
    for k in range(0, rows, 2):
        w0 = sf[pl.ds(k, nt, stride=rows), :] * c4
        w1 = sf[pl.ds(k + 1, nt, stride=rows), :] * c4
        s1[pl.ds(k * (nt // 8), nt // 4)] = jnp.concatenate([w0, w1], axis=0).astype(BF).reshape(nt // 4, 8, nj)

    pl.semaphore_wait(barrier, rows - 1 + nb - 1)

    def exchange(stage, n, peer, src_of, dst, me):
        def send(s, _):
            i, dev = peer(s)
            pltpu.make_async_remote_copy(
                src_ref=src_of(i), dst_ref=dst, send_sem=ssem.at[stage], recv_sem=rsem.at[stage],
                device_id=dev, device_id_type=MESH).start()
            return 0
        lax.fori_loop(1, n, send, 0)
        pltpu.make_async_copy(src_of(me), dst, rsem.at[stage]).start()

    def arrived(stage, buf):
        pltpu.make_async_copy(buf, buf, rsem.at[stage]).wait()

    def sent(stage, part):
        pltpu.make_async_copy(part, part, ssem.at[stage]).wait()

    u = nt // 8
    exchange(0, rows, row_peer, lambda i: s1.at[pl.ds(i * u, u)], r1.at[pl.ds(me_row * u, u)], me_row)

    loads[2].wait()
    n_deg = pn.deg
    owner = jnp.broadcast_to(dv[...], (128, n_deg)).T
    lanes = min(128, n_deg)
    owner = owner[:, :lanes]
    for c in range(n_deg // lanes):
        lane = lax.broadcasted_iota(jnp.int32, (n_deg, lanes), 1) + c * lanes
        hit = jnp.logical_and(owner == lane, lane >= order[0])
        perm[:, c * lanes:(c + 1) * lanes] = jnp.where(hit, 1.0, 0.0).astype(F32).astype(BF)
    loads[3].wait()
    qb = min(128, n_deg)

    def permute(i, _):
        q = pl.multiple_of(i * qb, qb)
        block = jnp.dot(perm[pl.ds(q, qb), :], tv[0], preferred_element_type=F32).astype(BF)
        tp[pl.ds(q, qb), :] = block
        tt[:, pl.ds(q, qb)] = block.T
        return 0

    lax.fori_loop(0, n_deg // qb, permute, 0)

    arrived(0, r1)
    sg = max(1, na // 4)
    columns = r1[...].reshape(rows * nt, nj)
    for i in range(na // sg):
        block = jnp.dot(tp[pl.ds(i * sg * nb, sg * nb), :], columns, preferred_element_type=F32)
        sp[pl.ds(i * sg, sg)] = block.astype(BF).reshape(sg, nb, nj)
    exchange(1, na, a_peer, lambda i: sp.at[i], e1.at[me_a], me_a)

    loads[4].wait()
    cg = min(4, cols)
    nr, nn = cg * pn.rd, cg * nj
    n_id = lax.broadcasted_iota(jnp.int32, (nr, nn), 1)
    r_id = lax.broadcasted_iota(jnp.int32, (nr, nn), 0)
    spread = jnp.where(r_id == (n_id // nj) * pn.rd + n_id % pn.rd, 1.0, 0.0).astype(F32).astype(BF)
    fc_id = (lax.broadcasted_iota(jnp.int32, (1, nn), 1) % nj) // pn.rd

    def widen(g, _):
        part = iv[0, pl.ds(pl.multiple_of(g * nr, nr), nr), :]
        x = lax.dot_general(part, spread, (((0,), (0,)), ((), ())), preferred_element_type=F32)
        for f in range(pn.fc):
            z = jnp.where(fc_id == f, x, 0.0).astype(BF)
            w[:, f, :, pl.ds(pl.multiple_of(g * nn, nn), nn)] = z.reshape(cols, pn.rd, nn)
        return 0

    lax.fori_loop(0, cols // cg, widen, 0)

    arrived(1, e1)
    sf[pl.ds(0, na * nb), :] = e1[...].reshape(na * nb, nj).astype(F32)
    for b in range(nb):
        e2[b] = sf[pl.ds(b, na, stride=nb), :].astype(BF)
    corner = d2.at[pl.ds(pl.multiple_of(xl * na, na), na), pl.ds(pl.multiple_of(me_col * nj, nj), nj)]
    exchange(2, nb, b_peer, lambda i: e2.at[i], corner, me_b)

    arrived(2, d2)
    for g in range(cols // cg):
        right = w[:, :, :, g * nn:(g + 1) * nn].reshape(cols * nj, nn)
        o2[:, g * nn:(g + 1) * nn] = jnp.dot(d2[...], right, preferred_element_type=F32).astype(BF)

    def tile_of(b):
        return o2.at[pl.ds(pl.multiple_of((b % pn.xl) * na, na), na),
                     pl.ds(pl.multiple_of((b // pn.xl) * nj, nj), nj)]

    exchange(3, nb, b_peer, tile_of, g1.at[me_b], me_b)
    arrived(3, g1)
    sf[pl.ds(0, na * nb), :] = g1[...].reshape(na * nb, nj).astype(F32)
    for a in range(na):
        g2[a] = sf[pl.ds(a, nb, stride=na), :].astype(BF)
    exchange(4, na, a_peer, lambda i: g2.at[i], h1.at[me_a], me_a)

    arrived(4, h1)
    coeffs = h1[...].reshape(n_deg, nj)
    lg = rows * nt // 4
    for i in range(4):
        block = jnp.dot(tt[pl.ds(i * lg, lg), :], coeffs, preferred_element_type=F32)
        ob[pl.ds(i * lg // 8, lg // 8)] = block.astype(BF).reshape(lg // 8, 8, nj)
    exchange(5, rows, row_peer, lambda i: ob.at[pl.ds(i * u, u)], vb.at[pl.ds(me_row * u, u)], me_row)

    arrived(5, vb)
    sf[...] = vb[...].reshape(rows * nt, nj).astype(F32)
    eye_j = (lax.broadcasted_iota(jnp.int32, (nj, nj), 0)
             == lax.broadcasted_iota(jnp.int32, (nj, nj), 1)).astype(F32).astype(BF)
    for t in range(nt):
        z = sf[pl.ds(t, rows, stride=nt), :].astype(BF)
        zv[t] = lax.dot_general(eye_j, z, (((1,), (1,)), ((), ())), preferred_element_type=F32).astype(BF)
    done = pltpu.make_async_copy(zv, out, insem.at[0])
    done.start()
    sent(0, s1.at[pl.ds(0, (rows - 1) * u)])
    sent(1, sp.at[pl.ds(0, na - 1)])
    sent(2, e2.at[pl.ds(0, nb - 1)])
    sent(3, g1.at[pl.ds(0, nb - 1)])
    sent(4, g2.at[pl.ds(0, na - 1)])
    sent(5, ob.at[pl.ds(0, (rows - 1) * u)])
    done.wait()


def solution(mesh):
    rows, cols = mesh.shape["row"], mesh.shape["col"]

    def per_device(field, coef, table, order_ids, inverses, degree_owner):
        orders, nt, f, c, rd = field.shape
        pn = Plan(rows, cols, table.shape[2], rd * cols, f * c)
        na, nb, nj, n_deg = pn.na, pn.nb, pn.j, pn.deg
        lat = rows * nt
        field = jnp.transpose(field, (1, 2, 3, 4, 0)).reshape(nt, nj, orders)
        deg = degree_owner.reshape(pn.y, pn.xl, pn.co, cols)
        deg = jnp.transpose(deg, (0, 2, 3, 1)).reshape(1, n_deg)
        anyspace = pl.BlockSpec(memory_space=pl.ANY)
        out = pl.pallas_call(
            functools.partial(kernel, pn),
            out_shape=jax.ShapeDtypeStruct((nt, nj, orders), BF),
            in_specs=[anyspace] * 5 + [pl.BlockSpec(memory_space=pltpu.SMEM)],
            out_specs=anyspace,
            scratch_shapes=[
                pltpu.VMEM((nt, nj, orders), BF),
                pltpu.VMEM((nt, rd), F32),
                pltpu.VMEM((1, n_deg, lat), BF),
                pltpu.VMEM((1, cols * rd, cols * rd), BF),
                pltpu.VMEM((1, n_deg), jnp.int32),
                pltpu.VMEM((lat // 8, 8, nj), BF),
                pltpu.VMEM((lat // 8, 8, nj), BF),
                pltpu.VMEM((lat, nj), F32),
                pltpu.VMEM((n_deg, n_deg), BF),
                pltpu.VMEM((n_deg, lat), BF),
                pltpu.VMEM((lat, n_deg), BF),
                pltpu.VMEM((cols, pn.fc, rd, cols * nj), BF),
                pltpu.VMEM((na, nb, nj), BF),
                pltpu.VMEM((na, nb, nj), BF),
                pltpu.VMEM((nb, na, nj), BF),
                pltpu.VMEM((rows, cols * nj), BF),
                pltpu.VMEM((rows, cols * nj), BF),
                pltpu.VMEM((nb, na, nj), BF),
                pltpu.VMEM((na, nb, nj), BF),
                pltpu.VMEM((na, nb, nj), BF),
                pltpu.VMEM((lat // 8, 8, nj), BF),
                pltpu.VMEM((lat // 8, 8, nj), BF),
                pltpu.VMEM((nt, nj, orders), BF),
                pltpu.SemaphoreType.DMA((5,)),
                pltpu.SemaphoreType.DMA((6,)),
                pltpu.SemaphoreType.DMA((6,)),
            ],
            compiler_params=pltpu.CompilerParams(
                collective_id=0, has_side_effects=True, vmem_limit_bytes=60 << 20),
        )(field, coef, table, inverses, deg, order_ids)
        out = out.reshape(nt, f, c, rd, orders)
        return jnp.transpose(out, (4, 0, 1, 2, 3))

    in_specs = (
        P(None, "row", None, None, "col"),
        P("row", "col"),
        P("row", None, None),
        P("row"),
        P(("row", "col"), None, None),
        P(),
    )
    return jax.shard_map(
        per_device, mesh=mesh, in_specs=in_specs,
        out_specs=P(None, "row", None, None, "col"), check_vma=False)
```

time: 221 us -> 94.9 us (0.43)
  blocking collectives: 95.1 us -> 0 us
  Pallas kernels: 0 us -> 90.3 us
  local copies, waits for them, and re-layouts: 48.6 us -> 3.76 us
  starting transfers between devices: 25.4 us -> 0 us
  waiting for transfers between devices: 24.6 us -> 0 us
  other arithmetic: 14 us -> 0 us
  matrix products: 10.8 us -> 0 us
    all_to_all x4 -> x0, blocking collectives: 95.1 us -> none  [the longest x1 25.9 us: per_device(): lax.all_to_all(placed, 'row', split_axis=1, concat_axis=0, tiled=True)]
    pallas_call x0 -> x1, Pallas kernels: none -> 90.3 us  [per_device(): pl.pallas_call(functools.partial(kernel, pn), out_shape=jax.ShapeDtypeStr...]
    all_to_all x2 -> x0, starting transfers between devices: 25.4 us -> none  [the longest x1 18.2 us: per_device(): lax.all_to_all(weighted, 'row', split_axis=0, concat_axis=1, tiled=True)]
    all_to_all x2 -> x0, waiting for transfers between devices: 24.6 us -> none  [the longest x1 15.5 us: per_device(): lax.all_to_all(weighted, 'row', split_axis=0, concat_axis=1, tiled=True)]
    gather x2 -> x0, local copies, waits for them, and re-layouts: 13.3 us -> none  [the longest x1 8.47 us: per_device(): coeffs = jnp.take(returned, inverse_order, axis=1)]
    unnamed x17 -> x1, local copies, waits for them, and re-layouts: 13.8 us -> 2.09 us
    dot_general x9 -> x0, matrix products: 10.8 us -> none  [the longest x4 5.24 us: synthesize_add_block(): lax.dot_general(table_part, coeff_part, (((0,), (0,)), ((), ())), preferr...]
    all_to_all x8 -> x0, local copies, waits for them, and re-layouts: 9.15 us -> none  [the longest x1 2.75 us: per_device(): lax.all_to_all(outputs, 'row', split_axis=1, concat_axis=0, tiled=True)]
  transfers between devices with their start and end apart: 2 -> 0, of which waited for: 2 -> 0; matrix products, arithmetic and copies ran while one was open for 2% -> 0% of each run, Pallas kernels for 0% -> 0%
where the time goes in v1:
time: 94.9 us; the launch traced here: 94.7 us
  Pallas kernels  90.3 us (95%)
  local copies, waits for them, and re-layouts  3.76 us (4%)
    pallas_call x1, Pallas kernels, per_device(): pl.pallas_call(functools.partial(kernel, pn), out_shape=jax.ShapeDtypeStr...  90.3 us
    unnamed x1, local copies, waits for them, and re-layouts  2.09 us

profile of v1, /device:TPU:1, one launch (start us, length us, event | category | flops | bytes accessed | tf_op | source)
XLA Modules:
  0.0 94.7 jit_solution(16552023640876638011)
XLA Ops:
  0.7 0.8 reshape.13
  1.4 0.2 copy.7
  1.6 0.7 reshape.14.deg
  2.3 90.3 %shard_map.64 = bf16[24,128,64]{2,1,0:T(8,128)(2,1)} custom-call(bf16[24,128,64]{2,1,0:T(8,128)(2,1)} %bitcast.10, f32[24,32]{1,0:T(8,128)} %coef.1, bf16[1,1024,1536]{2,1,0:T(8,128)(2,1)} %table.1, bf16[1,512,512]{2,1,0:T(8,128)(2,1)} %inv.1, s32[1,1024]{1,0:T(1,128)} %reshape.14.deg, s32[1]{0:T(128)S(6)} %copy.9.order), custom_call_target="tpu_custom_call" | custom-call | tf_op jit(solution)/shard_map/pallas_call | solution.py:212
  92.6 2.1 %copy.10 = bf16[64,24,2,2,32]{0,4,3,2,1:T(8,128)(2,1)} copy(bf16[64,24,2,2,32]{0,4,3,2,1:T(8,128)(2,1)} %bitcast.9) | data formatting | bytes 786432

commit v2 on v1

v2 whole, which is shorter than its diff:
```python
import functools

import jax
import jax.numpy as jnp
from jax import lax
from jax.experimental import pallas as pl
from jax.experimental.pallas import tpu as pltpu
from jax.sharding import PartitionSpec as P

MESH = pl.DeviceIdType.MESH
BF = jnp.bfloat16
F32 = jnp.float32


class Plan:
    def __init__(self, rows, cols, lat, radii, members):
        self.rows, self.cols = rows, cols
        self.co = 2
        self.xl = 4 if rows % 32 == 0 else 2
        self.y = rows // (self.xl * self.co)
        self.na = self.y * self.co
        self.nb = cols * self.xl
        self.deg = rows * cols
        self.t = lat // rows
        self.rd = radii // cols
        self.fc = members
        self.j = members * self.rd


def one_hot(hit):
    return jnp.where(hit, 1.0, 0.0).astype(F32).astype(BF)


def iota(shape, dim):
    return lax.broadcasted_iota(jnp.int32, shape, dim)


def kernel(pn, field, coef, table, inv, deg, order, out,
           fv, cv, tv, iv, dv, s1, r1, sf, perm, tp, tt, w, sp, e1, e2, d2, o2,
           g1, g2, h1, ob, insem, ssem, rsem):
    rows, cols, na, nb, nt, nj = pn.rows, pn.cols, pn.na, pn.nb, pn.t, pn.j
    ny, nx, nc, n_deg = pn.y, pn.xl, pn.co, pn.deg
    me_row, me_col = lax.axis_index("row"), lax.axis_index("col")
    co = me_row % nc
    xl = (me_row // nc) % nx
    y = me_row // (nc * nx)
    me_a = co * ny + y
    me_b = xl * cols + me_col
    u = nt // 8

    def row_dev(k):
        return (k, me_col)

    def a_dev(a):
        return (((a % ny) * nx + xl) * nc + a // ny, me_col)

    def b_dev(b):
        return ((y * nx + b // cols) * nc + co, b % cols)

    loads = [(field, fv), (coef, cv), (deg, dv), (table, tv), (inv, iv)]
    loads = [pltpu.make_async_copy(src, dst, insem.at[i]) for i, (src, dst) in enumerate(loads)]
    for c in loads:
        c.start()

    barrier = pltpu.get_barrier_semaphore()

    def greet_row(s, _):
        pl.semaphore_signal(barrier, inc=1, device_id=row_dev((me_row + s) % rows), device_id_type=MESH)
        return 0

    def greet_b(s, _):
        pl.semaphore_signal(barrier, inc=1, device_id=b_dev((me_b + s) % nb), device_id_type=MESH)
        return 0

    lax.fori_loop(1, rows, greet_row, 0)
    lax.fori_loop(1, nb, greet_b, 0)

    def put(src, dst, stage, half, dev, own):
        @pl.when(own)
        def _():
            pltpu.make_async_copy(src, dst, rsem.at[stage, half]).start()

        @pl.when(jnp.logical_not(own))
        def _():
            pltpu.make_async_remote_copy(
                src_ref=src, dst_ref=dst, send_sem=ssem.at[stage, half], recv_sem=rsem.at[stage, half],
                device_id=dev, device_id_type=MESH).start()

    def arrived(buf, stage, half):
        pltpu.make_async_copy(buf, buf, rsem.at[stage, half]).wait()

    def sent(part, stage, half):
        pltpu.make_async_copy(part, part, ssem.at[stage, half]).wait()

    loads[0].wait()
    loads[1].wait()
    eye = one_hot(iota((rows, rows), 0) == iota((rows, rows), 1))
    tc = 4
    for i in range(nt // tc):
        x = fv[pl.ds(i * tc, tc)].reshape(tc * nj, rows)
        yv = lax.dot_general(eye, x, (((1,), (1,)), ((), ())), preferred_element_type=F32)
        for t in range(tc):
            sf[pl.ds((i * tc + t) * rows, rows), :] = yv[:, t * nj:(t + 1) * nj]
    c4 = jnp.concatenate([cv[...]] * pn.fc, axis=1)
    pl.semaphore_wait(barrier, rows - 1 + nb - 1)
    chips = rows // nc

    for h in range(nc):
        def weigh(s, _):
            k = (me_row // nc + s) % chips * nc + h
            s1[pl.ds(k * u, u)] = (sf[pl.ds(k, nt, stride=rows), :] * c4).astype(BF).reshape(u, 8, nj)
            put(s1.at[pl.ds(k * u, u)], r1.at[pl.ds(me_row * u, u)], 0, 0, row_dev(k), k == me_row)
            return 0

        lax.fori_loop(0, chips, weigh, 0)

    loads[2].wait()
    lanes = min(128, n_deg)
    owner = jnp.broadcast_to(dv[...].reshape(1, n_deg), (128, n_deg)).T[:, :lanes]
    owner = jnp.concatenate(
        [owner[((v * nx + i) * nc + h) * cols:((v * nx + i) * nc + h + 1) * cols]
         for h in range(nc) for v in range(ny) for i in range(nx)], axis=0)
    for c in range(n_deg // lanes):
        lane = iota((n_deg, lanes), 1) + c * lanes
        perm[:, c * lanes:(c + 1) * lanes] = one_hot(jnp.logical_and(owner == lane, lane >= order[0]))
    loads[3].wait()
    qb = min(128, n_deg)

    def permute(i, _):
        q = pl.multiple_of(i * qb, qb)
        block = jnp.dot(perm[pl.ds(q, qb), :], tv[0], preferred_element_type=F32).astype(BF)
        tp[pl.ds(q, qb), :] = block
        tt[:, pl.ds(q, qb)] = block.T
        return 0

    lax.fori_loop(0, n_deg // qb, permute, 0)

    loads[4].wait()
    cg = min(4, cols)
    groups = cols // cg
    nr, nn = cg * pn.rd, cg * nj
    n_id, r_id = iota((nr, nn), 1), iota((nr, nn), 0)
    spread = one_hot(r_id == (n_id // nj) * pn.rd + n_id % pn.rd)
    fc_id = (iota((1, nn), 1) % nj) // pn.rd

    def widen(g, _):
        part = iv[0, pl.ds(pl.multiple_of(g * nr, nr), nr), :]
        x = lax.dot_general(part, spread, (((0,), (0,)), ((), ())), preferred_element_type=F32)
        for f in range(pn.fc):
            z = jnp.where(fc_id == f, x, 0.0).astype(BF)
            w[:, f, :, pl.ds(pl.multiple_of(g * nn, nn), nn)] = z.reshape(cols, pn.rd, nn)
        return 0

    lax.fori_loop(0, groups, widen, 0)

    arrived(r1, 0, 0)
    columns = r1[...].reshape(rows * nt, nj)
    for h in range(nc):
        block = jnp.dot(tp[pl.ds(h * ny * nb, ny * nb), :], columns, preferred_element_type=F32)
        sp[pl.ds(h * ny, ny)] = block.astype(BF).reshape(ny, nb, nj)

        def send_a(s, _):
            a = (y + s) % ny + h * ny
            for half in range(nc):
                @pl.when(co == half)
                def _():
                    put(sp.at[a], e1.at[me_a], 1, half, a_dev(a), a == me_a)
            return 0

        lax.fori_loop(0, ny, send_a, 0)

    for h in range(nc):
        arrived(e1.at[pl.ds(h * ny, ny)], 1, h)
        sf[pl.ds(0, ny * nb), :] = e1[pl.ds(h * ny, ny)].reshape(ny * nb, nj).astype(F32)
        corner = d2.at[h, xl, :, pl.ds(pl.multiple_of(me_col * nj, nj), nj)]

        def send_b(s, _):
            b = (me_b + s) % nb
            e2[h, b] = sf[pl.ds(b, ny, stride=nb), :].astype(BF)
            put(e2.at[h, b], corner, 2, h, b_dev(b), b == me_b)
            return 0

        lax.fori_loop(0, nb, send_b, 0)

    for h in range(nc):
        arrived(d2.at[h], 2, h)
        left = d2[h].reshape(nx * ny, cols * nj)
        for i in range(groups):
            g = (me_col // cg + i) % groups
            span = pl.ds(pl.multiple_of(g * nn, nn), nn)
            right = w[:, :, :, span].reshape(cols * nj, nn)
            part = jnp.dot(left, right, preferred_element_type=F32).astype(BF)
            o2[h, :, :, span] = part.reshape(nx, ny, nn)

            def send_back(s, _):
                xd = (xl + s // cg) % nx
                cd = g * cg + (me_col + s) % cg
                src = o2.at[h, xd, :, pl.ds(pl.multiple_of(cd * nj, nj), nj)]
                b = xd * cols + cd
                put(src, g1.at[h, me_b], 3, h, b_dev(b), b == me_b)
                return 0

            lax.fori_loop(0, nx * cg, send_back, 0)

    for h in range(nc):
        arrived(g1.at[h], 3, h)
        sf[pl.ds(0, ny * nb), :] = g1[h].reshape(ny * nb, nj).astype(F32)

        def send_home(s, _):
            v = (y + s) % ny
            a = h * ny + v
            g2[a] = sf[pl.ds(v, nb, stride=ny), :].astype(BF)
            put(g2.at[a], h1.at[me_a], 4, 0, a_dev(a), a == me_a)
            return 0

        lax.fori_loop(0, ny, send_home, 0)

    arrived(h1, 4, 0)
    coeffs = h1[...].reshape(n_deg, nj)
    parts = 4
    kg = rows // parts
    lg = kg * nt
    for i in range(parts):
        g = (me_row // kg + i) % parts
        rows_of = pl.ds(pl.multiple_of(g * lg, lg), lg)
        block = jnp.dot(tt[rows_of, :], coeffs, preferred_element_type=F32)
        ob[pl.ds(g * (lg // 8), lg // 8)] = block.astype(BF).reshape(lg // 8, 8, nj)

        def send_out(s, _):
            k = g * kg + (me_row + s) % kg
            put(ob.at[pl.ds(k * u, u)], out.at[pl.ds(me_row * u, u)], 5, 0, row_dev(k), k == me_row)
            return 0

        lax.fori_loop(0, kg, send_out, 0)

    sent(s1.at[pl.ds(0, (rows - 1) * u)], 0, 0)
    for half in range(nc):
        @pl.when(co == half)
        def _():
            sent(sp.at[pl.ds(0, na - 1)], 1, half)
        sent(e2.at[half, pl.ds(0, nb - 1)], 2, half)
        sent(g1.at[half, pl.ds(0, nb - 1)], 3, half)
    sent(g2.at[pl.ds(0, na - 1)], 4, 0)
    sent(ob.at[pl.ds(0, (rows - 1) * u)], 5, 0)
    arrived(out, 5, 0)


def unfold(v, out, sf):
    rows, _, nt, nj = v.shape
    sf[...] = v[:, 0].reshape(rows * nt, nj).astype(F32)
    eye = one_hot(iota((nj, nj), 0) == iota((nj, nj), 1))
    for t in range(nt):
        z = sf[pl.ds(t, rows, stride=nt), :].astype(BF)
        out[t] = lax.dot_general(eye, z, (((1,), (1,)), ((), ())), preferred_element_type=F32).astype(BF)


def solution(mesh):
    rows, cols = mesh.shape["row"], mesh.shape["col"]

    def per_device(field, coef, table, order_ids, inverses, degree_owner):
        orders, nt, f, c, rd = field.shape
        pn = Plan(rows, cols, table.shape[2], rd * cols, f * c)
        na, nb, nj, n_deg = pn.na, pn.nb, pn.j, pn.deg
        lat = rows * nt
        field = jnp.transpose(field, (1, 2, 3, 4, 0)).reshape(nt, nj, orders)
        anyspace = pl.BlockSpec(memory_space=pl.ANY)
        half = (pn.co, pn.xl, pn.y, cols * nj)
        out = pl.pallas_call(
            functools.partial(kernel, pn),
            out_shape=jax.ShapeDtypeStruct((lat // 8, 8, nj), BF),
            in_specs=[anyspace] * 5 + [pl.BlockSpec(memory_space=pltpu.SMEM)],
            out_specs=anyspace,
            scratch_shapes=[
                pltpu.VMEM((nt, nj, orders), BF),
                pltpu.VMEM((nt, rd), F32),
                pltpu.VMEM((1, n_deg, lat), BF),
                pltpu.VMEM((1, cols * rd, cols * rd), BF),
                pltpu.VMEM((n_deg,), jnp.int32),
                pltpu.VMEM((lat // 8, 8, nj), BF),
                pltpu.VMEM((lat // 8, 8, nj), BF),
                pltpu.VMEM((lat, nj), F32),
                pltpu.VMEM((n_deg, n_deg), BF),
                pltpu.VMEM((n_deg, lat), BF),
                pltpu.VMEM((lat, n_deg), BF),
                pltpu.VMEM((cols, pn.fc, rd, cols * nj), BF),
                pltpu.VMEM((na, nb, nj), BF),
                pltpu.VMEM((na, nb, nj), BF),
                pltpu.VMEM((pn.co, nb, pn.y, nj), BF),
                pltpu.VMEM(half, BF),
                pltpu.VMEM(half, BF),
                pltpu.VMEM((pn.co, nb, pn.y, nj), BF),
                pltpu.VMEM((na, nb, nj), BF),
                pltpu.VMEM((na, nb, nj), BF),
                pltpu.VMEM((lat // 8, 8, nj), BF),
                pltpu.SemaphoreType.DMA((5,)),
                pltpu.SemaphoreType.DMA((6, 2)),
                pltpu.SemaphoreType.DMA((6, 2)),
            ],
            compiler_params=pltpu.CompilerParams(
                collective_id=0, has_side_effects=True, vmem_limit_bytes=60 << 20),
        )(field, coef, table, inverses, degree_owner, order_ids)
        out = pl.pallas_call(
            unfold,
            grid=(nt // 8,),
            out_shape=jax.ShapeDtypeStruct((nt, nj, orders), BF),
            in_specs=[pl.BlockSpec((orders, 1, 8, nj), lambda i: (0, i, 0, 0))],
            out_specs=pl.BlockSpec((8, nj, orders), lambda i: (i, 0, 0)),
            scratch_shapes=[pltpu.VMEM((orders * 8, nj), F32)],
        )(out.reshape(orders, nt // 8, 8, nj))
        out = out.reshape(nt, f, c, rd, orders)
        return jnp.transpose(out, (4, 0, 1, 2, 3))

    in_specs = (
        P(None, "row", None, None, "col"),
        P("row", "col"),
        P("row", None, None),
        P("row"),
        P(("row", "col"), None, None),
        P(),
    )
    return jax.shard_map(
        per_device, mesh=mesh, in_specs=in_specs,
        out_specs=P(None, "row", None, None, "col"), check_vma=False)
```

time: 94.9 us -> 88.1 us (0.928)
  local copies, waits for them, and re-layouts: 3.76 us -> 0 us
  Pallas kernels: 90.3 us -> 87.3 us
    pallas_call x1, Pallas kernels: 90.3 us -> 84.2 us  [per_device(): pl.pallas_call(functools.partial(kernel, pn), out_shape=jax.ShapeDtypeStr...]
    pallas_call x0 -> x1, Pallas kernels: none -> 3.09 us  [per_device(): pl.pallas_call(unfold, grid=(nt // 8,), out_shape=jax.ShapeDtypeStruct((n...]
    unnamed x1 -> x0, local copies, waits for them, and re-layouts: 2.09 us -> none
    reshape x2 -> x0, local copies, waits for them, and re-layouts: 1.5 us -> none  [the longest x1 0.78 us: per_device(): deg = degree_owner.reshape(pn.y, pn.xl, pn.co, cols)]
where the time goes in v2:
time: 88.1 us; the launch traced here: 88 us
  Pallas kernels  87.3 us (99%)
    pallas_call x1, Pallas kernels, per_device(): pl.pallas_call(functools.partial(kernel, pn), out_shape=jax.ShapeDtypeStr...  84.2 us
    pallas_call x1, Pallas kernels, per_device(): pl.pallas_call(unfold, grid=(nt // 8,), out_shape=jax.ShapeDtypeStruct((n...  3.09 us

profile of v2, /device:TPU:1, one launch (start us, length us, event | category | flops | bytes accessed | tf_op | source)
XLA Modules:
  0.0 88.0 jit_solution(7074857286022646470)
XLA Ops:
  0.7 84.2 %shard_map.64 = bf16[192,8,128]{2,1,0:T(8,128)(2,1)} custom-call(bf16[24,128,64]{2,1,0:T(8,128)(2,1)} %bitcast.8, f32[24,32]{1,0:T(8,128)} %coef.1, bf16[1,1024,1536]{2,1,0:T(8,128)(2,1)} %table.1, bf16[1,512,512]{2,1,0:T(8,128)(2,1)} %inv.1, s32[1024]{0:T(1024)} %deg.1, s32[1]{0:T(128)S(6)} %copy.7.order), custom_call_target="tpu_custom_call" | custom-call | tf_op jit(solution)/shard_map/pallas_call | solution.py:268
  84.9 3.1 %shard_map.65 = bf16[24,128,64]{2,1,0:T(8,128)(2,1)} custom-call(bf16[64,3,8,128]{3,2,1,0:T(8,128)(2,1)} %bitcast.7), custom_call_target="tpu_custom_call" | custom-call | tf_op jit(solution)/shard_map/pallas_call | solution.py:302

commit v3 on v2

--- a/solution.py
+++ b/solution.py
@@ -35,6 +35,31 @@
     return lax.broadcasted_iota(jnp.int32, shape, dim)
 
 
+def wrap(i, n):
+    return jnp.where(i >= n, i - n, i)
+
+
+def far(t, n):
+    return jnp.where(t % 2 == 1, n // 2 - (t + 1) // 2, n // 2 + t // 2)
+
+
+def far_list(n):
+    return [n // 2 - (t + 1) // 2 if t % 2 else n // 2 + t // 2 for t in range(n)]
+
+
+def regroup(blocks, width):
+    n = len(blocks)
+    group = iota((1, blocks[0].shape[1]), 1) // width
+    out = []
+    for f in range(n):
+        moved = [pltpu.roll(x, (p - f) % n * width, 1) if p != f else x for p, x in enumerate(blocks)]
+        y = moved[0]
+        for p in range(1, n):
+            y = jnp.where(group == p, moved[p], y)
+        out.append(y)
+    return out
+
+
 def kernel(pn, field, coef, table, inv, deg, order, out,
            fv, cv, tv, iv, dv, s1, r1, sf, perm, tp, tt, w, sp, e1, e2, d2, o2,
            g1, g2, h1, ob, insem, ssem, rsem):
@@ -48,15 +73,6 @@
     me_b = xl * cols + me_col
     u = nt // 8
 
-    def row_dev(k):
-        return (k, me_col)
-
-    def a_dev(a):
-        return (((a % ny) * nx + xl) * nc + a // ny, me_col)
-
-    def b_dev(b):
-        return ((y * nx + b // cols) * nc + co, b % cols)
-
     loads = [(field, fv), (coef, cv), (deg, dv), (table, tv), (inv, iv)]
     loads = [pltpu.make_async_copy(src, dst, insem.at[i]) for i, (src, dst) in enumerate(loads)]
     for c in loads:
@@ -64,27 +80,48 @@
 
     barrier = pltpu.get_barrier_semaphore()
 
+    def greet(dev):
+        pl.semaphore_signal(barrier, inc=1, device_id=dev, device_id_type=MESH)
+
+    nz, ring = cols // 2, 2 * nx
+    x8 = me_col % 2 * nx + xl
+    z = me_col // 2
+    across = []
+    for dx in far_list(ring):
+        xd = wrap(x8 + dx, ring)
+        across.append((xd % nx, xd // nx, (y * nx + xd % nx) * nc + co))
+    others = [wrap(xl + i, nx) for i in range(nx)]
+    lines = [(y * nx + xd) * nc + co for xd in others]
+    chips = rows // nc
+    chip = y * nx + xl
+
+    greet((chip * nc + 1 - co, me_col))
+
     def greet_row(s, _):
-        pl.semaphore_signal(barrier, inc=1, device_id=row_dev((me_row + s) % rows), device_id_type=MESH)
+        k = wrap(chip + s, chips) * nc
+        for h in range(nc):
+            greet((k + h, me_col))
         return 0
 
-    def greet_b(s, _):
-        pl.semaphore_signal(barrier, inc=1, device_id=b_dev((me_b + s) % nb), device_id_type=MESH)
+    lax.fori_loop(1, chips, greet_row, 0)
+    for line in lines[1:]:
+        greet((line, me_col))
+
+    def greet_b(j, _):
+        cd = wrap(me_col + j, cols)
+        for line in lines:
+            greet((line, cd))
         return 0
 
-    lax.fori_loop(1, rows, greet_row, 0)
-    lax.fori_loop(1, nb, greet_b, 0)
-
-    def put(src, dst, stage, half, dev, own):
-        @pl.when(own)
-        def _():
-            pltpu.make_async_copy(src, dst, rsem.at[stage, half]).start()
-
-        @pl.when(jnp.logical_not(own))
-        def _():
-            pltpu.make_async_remote_copy(
-                src_ref=src, dst_ref=dst, send_sem=ssem.at[stage, half], recv_sem=rsem.at[stage, half],
-                device_id=dev, device_id_type=MESH).start()
+    lax.fori_loop(1, cols, greet_b, 0)
+
+    def put(src, dst, stage, half, dev):
+        pltpu.make_async_remote_copy(
+            src_ref=src, dst_ref=dst, send_sem=ssem.at[stage, half], recv_sem=rsem.at[stage, half],
+            device_id=dev, device_id_type=MESH).start()
+
+    def keep(src, dst, stage, half):
+        pltpu.make_async_copy(src, dst, rsem.at[stage, half]).start()
 
     def arrived(buf, stage, half):
         pltpu.make_async_copy(buf, buf, rsem.at[stage, half]).wait()
@@ -103,16 +140,35 @@
             sf[pl.ds((i * tc + t) * rows, rows), :] = yv[:, t * nj:(t + 1) * nj]
     c4 = jnp.concatenate([cv[...]] * pn.fc, axis=1)
     pl.semaphore_wait(barrier, rows - 1 + nb - 1)
-    chips = rows // nc
-
-    for h in range(nc):
-        def weigh(s, _):
-            k = (me_row // nc + s) % chips * nc + h
-            s1[pl.ds(k * u, u)] = (sf[pl.ds(k, nt, stride=rows), :] * c4).astype(BF).reshape(u, 8, nj)
-            put(s1.at[pl.ds(k * u, u)], r1.at[pl.ds(me_row * u, u)], 0, 0, row_dev(k), k == me_row)
+
+    def weigh(k):
+        block = (sf[pl.ds(k, nt, stride=rows), :] * c4).astype(BF)
+        s1[pl.ds(k * u, u)] = block.reshape(u, 8, nj)
+        return s1.at[pl.ds(k * u, u)], r1.at[pl.ds(me_row * u, u)], 0, 0
+
+    def weigh_half(h):
+        def weigh_all(t, _):
+            v = wrap(y + far(t, ny), ny)
+            for xd in others:
+                k = (v * nx + xd) * nc + h
+                put(*weigh(k), (k, me_col))
             return 0
 
-        lax.fori_loop(0, chips, weigh, 0)
+        lax.fori_loop(0, ny - 1, weigh_all, 0)
+        for xd in others[1:]:
+            k = (y * nx + xd) * nc + h
+            put(*weigh(k), (k, me_col))
+
+        @pl.when(co == h)
+        def _():
+            keep(*weigh(me_row))
+
+        @pl.when(co != h)
+        def _():
+            k = chip * nc + h
+            put(*weigh(k), (k, me_col))
+
+    weigh_half(0)
 
     loads[2].wait()
     lanes = min(128, n_deg)
@@ -124,34 +180,33 @@
         lane = iota((n_deg, lanes), 1) + c * lanes
         perm[:, c * lanes:(c + 1) * lanes] = one_hot(jnp.logical_and(owner == lane, lane >= order[0]))
     loads[3].wait()
-    qb = min(128, n_deg)
+    qb = min(512, n_deg)
 
     def permute(i, _):
         q = pl.multiple_of(i * qb, qb)
-        block = jnp.dot(perm[pl.ds(q, qb), :], tv[0], preferred_element_type=F32).astype(BF)
-        tp[pl.ds(q, qb), :] = block
-        tt[:, pl.ds(q, qb)] = block.T
+        tp[pl.ds(q, qb), :] = jnp.dot(perm[pl.ds(q, qb), :], tv[0], preferred_element_type=F32).astype(BF)
         return 0
 
-    lax.fori_loop(0, n_deg // qb, permute, 0)
+    lax.fori_loop(0, 1, permute, 0)
+    for h in range(1, nc):
+        weigh_half(h)
+    lax.fori_loop(1, n_deg // qb, permute, 0)
 
     loads[4].wait()
-    cg = min(4, cols)
-    groups = cols // cg
-    nr, nn = cg * pn.rd, cg * nj
-    n_id, r_id = iota((nr, nn), 1), iota((nr, nn), 0)
-    spread = one_hot(r_id == (n_id // nj) * pn.rd + n_id % pn.rd)
-    fc_id = (iota((1, nn), 1) % nj) // pn.rd
-
-    def widen(g, _):
-        part = iv[0, pl.ds(pl.multiple_of(g * nr, nr), nr), :]
-        x = lax.dot_general(part, spread, (((0,), (0,)), ((), ())), preferred_element_type=F32)
-        for f in range(pn.fc):
-            z = jnp.where(fc_id == f, x, 0.0).astype(BF)
-            w[:, f, :, pl.ds(pl.multiple_of(g * nn, nn), nn)] = z.reshape(cols, pn.rd, nn)
+    tb = min(256, n_deg)
+
+    def turn(i, _):
+        q = pl.multiple_of(i * tb, tb)
+        tt[:, pl.ds(q, tb)] = tp[pl.ds(q, tb), :].T
         return 0
 
-    lax.fori_loop(0, groups, widen, 0)
+    def prepare():
+        w[...] = iv[0].T
+        lax.fori_loop(0, n_deg // tb, turn, 0)
+
+    @pl.when(co != 0)
+    def _():
+        prepare()
 
     arrived(r1, 0, 0)
     columns = r1[...].reshape(rows * nt, nj)
@@ -159,80 +214,124 @@
         block = jnp.dot(tp[pl.ds(h * ny * nb, ny * nb), :], columns, preferred_element_type=F32)
         sp[pl.ds(h * ny, ny)] = block.astype(BF).reshape(ny, nb, nj)
 
-        def send_a(s, _):
-            a = (y + s) % ny + h * ny
-            for half in range(nc):
-                @pl.when(co == half)
-                def _():
-                    put(sp.at[a], e1.at[me_a], 1, half, a_dev(a), a == me_a)
+        for half in range(nc):
+            @pl.when(co == half)
+            def _():
+                def send_a(v, h=h, half=half):
+                    a = h * ny + v
+                    return sp.at[a], e1.at[me_a], 1, half
+
+                def send_all(t, _):
+                    v = wrap(y + far(t, ny), ny)
+                    put(*send_a(v), ((v * nx + xl) * nc + h, me_col))
+                    return 0
+
+                lax.fori_loop(0, ny - 1, send_all, 0)
+                if half == h:
+                    keep(*send_a(y))
+                else:
+                    put(*send_a(y), (chip * nc + h, me_col))
+
+    @pl.when(co == 0)
+    def _():
+        prepare()
+
+    def to_b(block):
+        def line_of(t, _):
+            zd = wrap(z + far(t, nz), nz) * 2
+            for xd, hi, line in across:
+                put(*block(xd * cols + zd + hi), (line, zd + hi))
             return 0
 
-        lax.fori_loop(0, ny, send_a, 0)
+        lax.fori_loop(0, nz - 1, line_of, 0)
+        for xd, hi, line in across[:-1]:
+            put(*block(xd * cols + z * 2 + hi), (line, z * 2 + hi))
+        keep(*block(me_b))
 
     for h in range(nc):
         arrived(e1.at[pl.ds(h * ny, ny)], 1, h)
         sf[pl.ds(0, ny * nb), :] = e1[pl.ds(h * ny, ny)].reshape(ny * nb, nj).astype(F32)
         corner = d2.at[h, xl, :, pl.ds(pl.multiple_of(me_col * nj, nj), nj)]
 
-        def send_b(s, _):
-            b = (me_b + s) % nb
+        def send_b(b):
             e2[h, b] = sf[pl.ds(b, ny, stride=nb), :].astype(BF)
-            put(e2.at[h, b], corner, 2, h, b_dev(b), b == me_b)
-            return 0
-
-        lax.fori_loop(0, nb, send_b, 0)
+            return e2.at[h, b], corner, 2, h
+
+        to_b(send_b)
 
     for h in range(nc):
         arrived(d2.at[h], 2, h)
-        left = d2[h].reshape(nx * ny, cols * nj)
-        for i in range(groups):
-            g = (me_col // cg + i) % groups
-            span = pl.ds(pl.multiple_of(g * nn, nn), nn)
-            right = w[:, :, :, span].reshape(cols * nj, nn)
-            part = jnp.dot(left, right, preferred_element_type=F32).astype(BF)
-            o2[h, :, :, span] = part.reshape(nx, ny, nn)
-
-            def send_back(s, _):
-                xd = (xl + s // cg) % nx
-                cd = g * cg + (me_col + s) % cg
-                src = o2.at[h, xd, :, pl.ds(pl.multiple_of(cd * nj, nj), nj)]
-                b = xd * cols + cd
-                put(src, g1.at[h, me_b], 3, h, b_dev(b), b == me_b)
-                return 0
-
-            lax.fori_loop(0, nx * cg, send_back, 0)
+        left = d2[h].reshape(nx * ny, cols * nj).astype(F32)
+        fc, m = pn.fc, nx * ny
+        quads = [regroup([left[:, (g * fc + p) * nj:(g * fc + p + 1) * nj] for p in range(fc)], pn.rd)
+                 for g in range(cols // fc)]
+        left = jnp.concatenate(
+            [jnp.concatenate([quad[f] for quad in quads], axis=1) for f in range(fc)], axis=0).astype(BF)
+        right = jnp.dot(left, w[...], preferred_element_type=F32)
+        for g in range(cols // fc):
+            quad = regroup([right[f * m:(f + 1) * m, g * nj:(g + 1) * nj] for f in range(fc)], pn.rd)
+            for p in range(fc):
+                c = g * fc + p
+                o2[h, :, :, c * nj:(c + 1) * nj] = quad[p].astype(BF).reshape(nx, ny, nj)
+
+        def send_back(b, h=h):
+            src = o2.at[h, b // cols, :, pl.ds(pl.multiple_of(b % cols * nj, nj), nj)]
+            return src, g1.at[h, me_b], 3, h
+
+        to_b(send_back)
 
     for h in range(nc):
         arrived(g1.at[h], 3, h)
         sf[pl.ds(0, ny * nb), :] = g1[h].reshape(ny * nb, nj).astype(F32)
 
-        def send_home(s, _):
-            v = (y + s) % ny
+        def send_home(v, h=h):
             a = h * ny + v
             g2[a] = sf[pl.ds(v, nb, stride=ny), :].astype(BF)
-            put(g2.at[a], h1.at[me_a], 4, 0, a_dev(a), a == me_a)
+            return g2.at[a], h1.at[me_a], 4, 0
+
+        def send_homes(t, _):
+            v = wrap(y + far(t, ny), ny)
+            put(*send_home(v), ((v * nx + xl) * nc + h, me_col))
             return 0
 
-        lax.fori_loop(0, ny, send_home, 0)
+        lax.fori_loop(0, ny - 1, send_homes, 0)
+
+        @pl.when(co == h)
+        def _():
+            keep(*send_home(y))
+
+        @pl.when(co != h)
+        def _():
+            put(*send_home(y), (chip * nc + h, me_col))
 
     arrived(h1, 4, 0)
     coeffs = h1[...].reshape(n_deg, nj)
     parts = 4
     kg = rows // parts
     lg = kg * nt
-    for i in range(parts):
-        g = (me_row // kg + i) % parts
+    for i in far_list(parts):
+        g = wrap(me_row // kg + i, parts)
         rows_of = pl.ds(pl.multiple_of(g * lg, lg), lg)
         block = jnp.dot(tt[rows_of, :], coeffs, preferred_element_type=F32)
         ob[pl.ds(g * (lg // 8), lg // 8)] = block.astype(BF).reshape(lg // 8, 8, nj)
 
-        def send_out(s, _):
-            k = g * kg + (me_row + s) % kg
-            put(ob.at[pl.ds(k * u, u)], out.at[pl.ds(me_row * u, u)], 5, 0, row_dev(k), k == me_row)
+        def send_out(k):
+            return ob.at[pl.ds(k * u, u)], out.at[pl.ds(me_row * u, u)], 5, 0
+
+        first = me_row % kg
+        if i == 0:
+            keep(*send_out(me_row))
+        else:
+            put(*send_out(g * kg + first), (g * kg + first, me_col))
+
+        def send_outs(s, _):
+            k = g * kg + wrap(first + s, kg)
+            put(*send_out(k), (k, me_col))
             return 0
 
-        lax.fori_loop(0, kg, send_out, 0)
-
+        lax.fori_loop(1, kg, send_outs, 0)
+
+    arrived(out, 5, 0)
     sent(s1.at[pl.ds(0, (rows - 1) * u)], 0, 0)
     for half in range(nc):
         @pl.when(co == half)
@@ -242,7 +341,6 @@
         sent(g1.at[half, pl.ds(0, nb - 1)], 3, half)
     sent(g2.at[pl.ds(0, na - 1)], 4, 0)
     sent(ob.at[pl.ds(0, (rows - 1) * u)], 5, 0)
-    arrived(out, 5, 0)
 
 
 def unfold(v, out, sf):
@@ -282,7 +380,7 @@
                 pltpu.VMEM((n_deg, n_deg), BF),
                 pltpu.VMEM((n_deg, lat), BF),
                 pltpu.VMEM((lat, n_deg), BF),
-                pltpu.VMEM((cols, pn.fc, rd, cols * nj), BF),
+                pltpu.VMEM((cols * rd, cols * rd), BF),
                 pltpu.VMEM((na, nb, nj), BF),
                 pltpu.VMEM((na, nb, nj), BF),
                 pltpu.VMEM((pn.co, nb, pn.y, nj), BF),

time: 88.1 us -> 82.5 us (0.936)
  Pallas kernels: 87.3 us -> 81.7 us
    pallas_call x1, Pallas kernels: 84.2 us -> 78.6 us  [per_device(): pl.pallas_call(functools.partial(kernel, pn), out_shape=jax.ShapeDtypeStr...]
where the time goes in v3:
time: 82.5 us; the launch traced here: 82.4 us
  Pallas kernels  81.7 us (99%)
    pallas_call x1, Pallas kernels, per_device(): pl.pallas_call(functools.partial(kernel, pn), out_shape=jax.ShapeDtypeStr...  78.6 us
    pallas_call x1, Pallas kernels, per_device(): pl.pallas_call(unfold, grid=(nt // 8,), out_shape=jax.ShapeDtypeStruct((n...  3.09 us

profile of v3, /device:TPU:1, one launch (start us, length us, event | category | flops | bytes accessed | tf_op | source)
XLA Modules:
  0.0 82.4 jit_solution(10017270994272127983)
XLA Ops:
  0.7 78.6 %shard_map.64 = bf16[192,8,128]{2,1,0:T(8,128)(2,1)} custom-call(bf16[24,128,64]{2,1,0:T(8,128)(2,1)} %bitcast.8, f32[24,32]{1,0:T(8,128)} %coef.1, bf16[1,1024,1536]{2,1,0:T(8,128)(2,1)} %table.1, bf16[1,512,512]{2,1,0:T(8,128)(2,1)} %inv.1, s32[1024]{0:T(1024)} %deg.1, s32[1]{0:T(128)S(6)} %copy.7.order), custom_call_target="tpu_custom_call" | custom-call | tf_op jit(solution)/shard_map/pallas_call | solution.py:366
  79.3 3.1 %shard_map.65 = bf16[24,128,64]{2,1,0:T(8,128)(2,1)} custom-call(bf16[64,3,8,128]{3,2,1,0:T(8,128)(2,1)} %bitcast.7), custom_call_target="tpu_custom_call" | custom-call | tf_op jit(solution)/shard_map/pallas_call | solution.py:400

commit v4 on v3

--- a/solution.py
+++ b/solution.py
@@ -62,7 +62,7 @@
 
 def kernel(pn, field, coef, table, inv, deg, order, out,
            fv, cv, tv, iv, dv, s1, r1, sf, perm, tp, tt, w, sp, e1, e2, d2, o2,
-           g1, g2, h1, ob, insem, ssem, rsem):
+           g1, g2, h1, ob, ov, insem, ssem, rsem):
     rows, cols, na, nb, nt, nj = pn.rows, pn.cols, pn.na, pn.nb, pn.t, pn.j
     ny, nx, nc, n_deg = pn.y, pn.xl, pn.co, pn.deg
     me_row, me_col = lax.axis_index("row"), lax.axis_index("col")
@@ -73,7 +73,7 @@
     me_b = xl * cols + me_col
     u = nt // 8
 
-    loads = [(field, fv), (coef, cv), (deg, dv), (table, tv), (inv, iv)]
+    loads = [(field, fv), (coef, cv), (deg, dv), (table, tv), (inv, iv), (order, ov)]
     loads = [pltpu.make_async_copy(src, dst, insem.at[i]) for i, (src, dst) in enumerate(loads)]
     for c in loads:
         c.start()
@@ -91,29 +91,29 @@
         xd = wrap(x8 + dx, ring)
         across.append((xd % nx, xd // nx, (y * nx + xd % nx) * nc + co))
     others = [wrap(xl + i, nx) for i in range(nx)]
-    lines = [(y * nx + xd) * nc + co for xd in others]
-    chips = rows // nc
     chip = y * nx + xl
 
+    def greet_b(t, _):
+        zd = wrap(z + far(t, nz), nz) * 2
+        for _, hi, line in across:
+            greet((line, zd + hi))
+        return 0
+
+    def greet_row(t, _):
+        v = wrap(y + far(t, ny), ny)
+        for xd in others:
+            for h in range(nc):
+                greet(((v * nx + xd) * nc + h, me_col))
+        return 0
+
+    lax.fori_loop(0, nz - 1, greet_b, 0)
+    lax.fori_loop(0, ny - 1, greet_row, 0)
+    for _, hi, line in across[:-1]:
+        greet((line, z * 2 + hi))
+    for xd in others[1:]:
+        for h in range(nc):
+            greet(((y * nx + xd) * nc + h, me_col))
     greet((chip * nc + 1 - co, me_col))
-
-    def greet_row(s, _):
-        k = wrap(chip + s, chips) * nc
-        for h in range(nc):
-            greet((k + h, me_col))
-        return 0
-
-    lax.fori_loop(1, chips, greet_row, 0)
-    for line in lines[1:]:
-        greet((line, me_col))
-
-    def greet_b(j, _):
-        cd = wrap(me_col + j, cols)
-        for line in lines:
-            greet((line, cd))
-        return 0
-
-    lax.fori_loop(1, cols, greet_b, 0)
 
     def put(src, dst, stage, half, dev):
         pltpu.make_async_remote_copy(
@@ -171,6 +171,7 @@
     weigh_half(0)
 
     loads[2].wait()
+    loads[5].wait()
     lanes = min(128, n_deg)
     owner = jnp.broadcast_to(dv[...].reshape(1, n_deg), (128, n_deg)).T[:, :lanes]
     owner = jnp.concatenate(
@@ -178,7 +179,7 @@
          for h in range(nc) for v in range(ny) for i in range(nx)], axis=0)
     for c in range(n_deg // lanes):
         lane = iota((n_deg, lanes), 1) + c * lanes
-        perm[:, c * lanes:(c + 1) * lanes] = one_hot(jnp.logical_and(owner == lane, lane >= order[0]))
+        perm[:, c * lanes:(c + 1) * lanes] = one_hot(jnp.logical_and(owner == lane, lane >= ov[0]))
     loads[3].wait()
     qb = min(512, n_deg)
 
@@ -284,48 +285,53 @@
         arrived(g1.at[h], 3, h)
         sf[pl.ds(0, ny * nb), :] = g1[h].reshape(ny * nb, nj).astype(F32)
 
-        def send_home(v, h=h):
-            a = h * ny + v
-            g2[a] = sf[pl.ds(v, nb, stride=ny), :].astype(BF)
-            return g2.at[a], h1.at[me_a], 4, 0
-
-        def send_homes(t, _):
-            v = wrap(y + far(t, ny), ny)
-            put(*send_home(v), ((v * nx + xl) * nc + h, me_col))
-            return 0
-
-        lax.fori_loop(0, ny - 1, send_homes, 0)
-
-        @pl.when(co == h)
-        def _():
-            keep(*send_home(y))
-
-        @pl.when(co != h)
-        def _():
-            put(*send_home(y), (chip * nc + h, me_col))
-
-    arrived(h1, 4, 0)
-    coeffs = h1[...].reshape(n_deg, nj)
+        for half in range(nc):
+            @pl.when(co == half)
+            def _():
+                def send_home(v, h=h, half=half):
+                    a = h * ny + v
+                    g2[a] = sf[pl.ds(v, nb, stride=ny), :].astype(BF)
+                    return g2.at[a], h1.at[me_a], 4, half
+
+                def send_homes(t, _):
+                    v = wrap(y + far(t, ny), ny)
+                    put(*send_home(v), ((v * nx + xl) * nc + h, me_col))
+                    return 0
+
+                lax.fori_loop(0, ny - 1, send_homes, 0)
+                if half == h:
+                    keep(*send_home(y))
+                else:
+                    put(*send_home(y), (chip * nc + h, me_col))
+
     parts = 4
     kg = rows // parts
     lg = kg * nt
+    hq = ny * nb
+    arrived(h1.at[pl.ds(0, ny)], 4, 0)
+    first = h1[pl.ds(0, ny)].reshape(hq, nj)
+    for i in range(parts):
+        rows_of = pl.ds(i * lg, lg)
+        sf[rows_of, :] = jnp.dot(tt[rows_of, :hq], first, preferred_element_type=F32)
+    arrived(h1.at[pl.ds(ny, ny)], 4, 1)
+    second = h1[pl.ds(ny, ny)].reshape(hq, nj)
     for i in far_list(parts):
         g = wrap(me_row // kg + i, parts)
         rows_of = pl.ds(pl.multiple_of(g * lg, lg), lg)
-        block = jnp.dot(tt[rows_of, :], coeffs, preferred_element_type=F32)
+        block = sf[rows_of, :] + jnp.dot(tt[rows_of, hq:], second, preferred_element_type=F32)
         ob[pl.ds(g * (lg // 8), lg // 8)] = block.astype(BF).reshape(lg // 8, 8, nj)
 
         def send_out(k):
             return ob.at[pl.ds(k * u, u)], out.at[pl.ds(me_row * u, u)], 5, 0
 
-        first = me_row % kg
+        mine = me_row % kg
         if i == 0:
             keep(*send_out(me_row))
         else:
-            put(*send_out(g * kg + first), (g * kg + first, me_col))
+            put(*send_out(g * kg + mine), (g * kg + mine, me_col))
 
         def send_outs(s, _):
-            k = g * kg + wrap(first + s, kg)
+            k = g * kg + wrap(mine + s, kg)
             put(*send_out(k), (k, me_col))
             return 0
 
@@ -337,19 +343,18 @@
         @pl.when(co == half)
         def _():
             sent(sp.at[pl.ds(0, na - 1)], 1, half)
+            sent(g2.at[pl.ds(0, na - 1)], 4, half)
         sent(e2.at[half, pl.ds(0, nb - 1)], 2, half)
         sent(g1.at[half, pl.ds(0, nb - 1)], 3, half)
-    sent(g2.at[pl.ds(0, na - 1)], 4, 0)
     sent(ob.at[pl.ds(0, (rows - 1) * u)], 5, 0)
 
 
 def unfold(v, out, sf):
-    rows, _, nt, nj = v.shape
-    sf[...] = v[:, 0].reshape(rows * nt, nj).astype(F32)
-    eye = one_hot(iota((nj, nj), 0) == iota((nj, nj), 1))
+    rows, _, _, nj = v.shape
+    nt = out.shape[0]
+    sf[...] = v[...].reshape(rows * nt, nj).astype(F32)
     for t in range(nt):
-        z = sf[pl.ds(t, rows, stride=nt), :].astype(BF)
-        out[t] = lax.dot_general(eye, z, (((1,), (1,)), ((), ())), preferred_element_type=F32).astype(BF)
+        out[t] = sf[pl.ds(t, rows, stride=nt), :].T.astype(BF)
 
 
 def solution(mesh):
@@ -366,7 +371,7 @@
         out = pl.pallas_call(
             functools.partial(kernel, pn),
             out_shape=jax.ShapeDtypeStruct((lat // 8, 8, nj), BF),
-            in_specs=[anyspace] * 5 + [pl.BlockSpec(memory_space=pltpu.SMEM)],
+            in_specs=[anyspace] * 6,
             out_specs=anyspace,
             scratch_shapes=[
                 pltpu.VMEM((nt, nj, orders), BF),
@@ -390,7 +395,8 @@
                 pltpu.VMEM((na, nb, nj), BF),
                 pltpu.VMEM((na, nb, nj), BF),
                 pltpu.VMEM((lat // 8, 8, nj), BF),
-                pltpu.SemaphoreType.DMA((5,)),
+                pltpu.SMEM((1,), jnp.int32),
+                pltpu.SemaphoreType.DMA((6,)),
                 pltpu.SemaphoreType.DMA((6, 2)),
                 pltpu.SemaphoreType.DMA((6, 2)),
             ],
@@ -399,11 +405,11 @@
         )(field, coef, table, inverses, degree_owner, order_ids)
         out = pl.pallas_call(
             unfold,
-            grid=(nt // 8,),
+            grid=(1,),
             out_shape=jax.ShapeDtypeStruct((nt, nj, orders), BF),
-            in_specs=[pl.BlockSpec((orders, 1, 8, nj), lambda i: (0, i, 0, 0))],
-            out_specs=pl.BlockSpec((8, nj, orders), lambda i: (i, 0, 0)),
-            scratch_shapes=[pltpu.VMEM((orders * 8, nj), F32)],
+            in_specs=[pl.BlockSpec((orders, nt // 8, 8, nj), lambda i: (0, 0, 0, 0))],
+            out_specs=pl.BlockSpec((nt, nj, orders), lambda i: (0, 0, 0)),
+            scratch_shapes=[pltpu.VMEM((orders * nt, nj), F32)],
         )(out.reshape(orders, nt // 8, 8, nj))
         out = out.reshape(nt, f, c, rd, orders)
         return jnp.transpose(out, (4, 0, 1, 2, 3))

time: 82.5 us -> 79.9 us (0.968)
  Pallas kernels: 81.7 us -> 79 us
    pallas_call x1, Pallas kernels: 78.6 us -> 76.8 us  [per_device(): pl.pallas_call(functools.partial(kernel, pn), out_shape=jax.ShapeDtypeStr...]
    pallas_call x1, Pallas kernels: 3.09 us -> 2.18 us  [per_device(): pl.pallas_call(unfold, grid=(1,), out_shape=jax.ShapeDtypeStruct((nt, nj,...]
where the time goes in v4:
time: 79.9 us; the launch traced here: 79.7 us
  Pallas kernels  79 us (99%)
    pallas_call x1, Pallas kernels, per_device(): pl.pallas_call(functools.partial(kernel, pn), out_shape=jax.ShapeDtypeStr...  76.8 us
    pallas_call x1, Pallas kernels, per_device(): pl.pallas_call(unfold, grid=(1,), out_shape=jax.ShapeDtypeStruct((nt, nj,...  2.18 us

profile of v4, /device:TPU:1, one launch (start us, length us, event | category | flops | bytes accessed | tf_op | source)
XLA Modules:
  0.0 79.7 jit_solution(14795518281732310336)
XLA Ops:
  0.7 76.8 %shard_map.64 = bf16[192,8,128]{2,1,0:T(8,128)(2,1)} custom-call(bf16[24,128,64]{2,1,0:T(8,128)(2,1)} %bitcast.8, f32[24,32]{1,0:T(8,128)} %coef.1, bf16[1,1024,1536]{2,1,0:T(8,128)(2,1)} %table.1, bf16[1,512,512]{2,1,0:T(8,128)(2,1)} %inv.1, s32[1024]{0:T(1024)} %deg.1, s32[1]{0:T(128)S(6)} %copy.7.order), custom_call_target="tpu_custom_call" | custom-call | tf_op jit(solution)/shard_map/pallas_call | solution.py:371
  77.5 2.2 %shard_map.65 = bf16[24,128,64]{2,1,0:T(8,128)(2,1)} custom-call(bf16[64,3,8,128]{3,2,1,0:T(8,128)(2,1)} %bitcast.7), custom_call_target="tpu_custom_call" | custom-call | tf_op jit(solution)/shard_map/pallas_call | solution.py:406
